TPU v7x, 32 devices: a whole 2x2x4 slice. The times are simulated.
32 devices in a mesh: ctx: 4 (over y, x), grp: 4 (over z), side: 2 (over core).
Axes of the slice: x: 2, y: 2, z: 4, core: 2. Of those that a mesh axis runs over, the one named last changes fastest.
Arguments:
- tokens: bfloat16 [512, 2048], P(('ctx', 'grp', 'side')), may hold values from -6 to 6
- norm_gain: float32 [2048], replicated, may hold values from 0.25 to 1.75
- combine: float32 [512, 8], P(('ctx', 'grp', 'side')), may hold values from 0.05 to 0.6
- expert_ids: int32 [512, 8], P(('ctx', 'grp', 'side')), may hold values from 0 to 15, all different within a row; in each aligned block of 16 rows (0 to 15, 16 to 31, ...) at most 11 rows name the same one
- w_gate: bfloat16 [16, 2048, 768], P(('ctx', 'grp'), None, 'side'), may hold values from -0.125 to 0.125
- w_up: bfloat16 [16, 2048, 768], P(('ctx', 'grp'), None, 'side'), may hold values from -0.125 to 0.125
- w_down: bfloat16 [16, 768, 2048], P(('ctx', 'grp'), 'side'), may hold values from -0.21875 to 0.21875
- d_out: bfloat16 [512, 2048], P(('ctx', 'grp', 'side')), may hold values from -6 to 6
Outputs:
- mixed: bfloat16 [512, 2048], P(('ctx', 'grp', 'side'))
- d_tokens: bfloat16 [512, 2048], P(('ctx', 'grp', 'side'))
- d_gain: float32 [2048], replicated
- d_combine: float32 [512, 8], P(('ctx', 'grp', 'side'))
- d_w_gate: bfloat16 [16, 2048, 768], P(('ctx', 'grp'), None, 'side')
- d_w_up: bfloat16 [16, 2048, 768], P(('ctx', 'grp'), None, 'side')
- d_w_down: bfloat16 [16, 768, 2048], P(('ctx', 'grp'), 'side')
Inputs may be any that keep to these rules, and one draw needn't show every extreme that they name: `expert_ids`: each row names 8 different experts; among the 16 rows of one device no expert is named more than 11 times, and that bound is reached.
All inputs are finite; a program needn't handle non-finite values.
Results may differ from a plain program's by a relative error of at most 0.0072.
Values may be sent and summed in bfloat16 or wider, within the bound.
A program may use at most 128 MiB of HBM per device.

v0:
```python
import jax
import jax.numpy as jnp
from jax import lax
from jax.sharding import PartitionSpec as P

EPS = 1e-06


def expert_pass(rows, grads, gate_w, up_w, down_w):
    a_gate = jnp.dot(rows, gate_w, preferred_element_type=jnp.float32)
    a_up = jnp.dot(rows, up_w, preferred_element_type=jnp.float32)
    sigmoid_gate = jax.nn.sigmoid(a_gate)
    silu_gate = a_gate * sigmoid_gate
    hidden = (silu_gate * a_up).astype(jnp.bfloat16)
    output = jnp.dot(hidden, down_w, preferred_element_type=jnp.float32)
    d_hidden = lax.dot_general(
        grads, down_w, (((1,), (1,)), ((), ())), preferred_element_type=jnp.float32
    )
    d_up = (d_hidden * silu_gate).astype(jnp.bfloat16)
    d_gate = (d_hidden * a_up * sigmoid_gate * (1.0 + a_gate * (1.0 - sigmoid_gate))).astype(
        jnp.bfloat16
    )
    d_rows = lax.dot_general(
        d_gate, gate_w, (((1,), (1,)), ((), ())), preferred_element_type=jnp.float32
    )
    d_rows = d_rows + lax.dot_general(
        d_up, up_w, (((1,), (1,)), ((), ())), preferred_element_type=jnp.float32
    )
    g_gate = lax.dot_general(
        rows, d_gate, (((0,), (0,)), ((), ())), preferred_element_type=jnp.float32
    )
    g_up = lax.dot_general(rows, d_up, (((0,), (0,)), ((), ())), preferred_element_type=jnp.float32)
    g_down = lax.dot_general(
        hidden, grads, (((0,), (0,)), ((), ())), preferred_element_type=jnp.float32
    )
    return (output, d_rows, g_gate, g_up, g_down)


def local(tokens, norm_gain, combine, expert_ids, w_gate, w_up, w_down, d_out):
    count = tokens.shape[0]
    width = tokens.shape[1]
    chosen = expert_ids.shape[1]
    n_ctx = lax.axis_size("ctx")
    n_grp = lax.axis_size("grp")
    experts = n_ctx * n_grp
    slots = max(2, (4 * count * chosen + 3 * experts - 1) // (3 * experts))
    places = experts * slots
    x_float = tokens.astype(jnp.float32)
    inv_rms = lax.rsqrt(jnp.mean(x_float * x_float, axis=1, keepdims=True) + EPS)
    normed = (x_float * inv_rms * norm_gain).astype(jnp.bfloat16)
    grad_float = d_out.astype(jnp.float32)
    flat_ids = expert_ids.reshape(-1)
    onehot = (flat_ids[:, None] == jnp.arange(experts, dtype=jnp.int32)[None, :]).astype(jnp.int32)
    before = jnp.cumsum(onehot, axis=0) - onehot
    slot = jnp.sum(before * onehot, axis=1)
    target = flat_ids * slots + slot
    select = (target[:, None] == jnp.arange(places, dtype=jnp.int32)[None, :]).astype(jnp.float32)
    per_token = select.reshape(count, chosen, places)
    token_map = jnp.sum(per_token, axis=1).astype(jnp.bfloat16)
    weighted = jnp.sum(per_token * combine[:, :, None], axis=1)
    send_rows = lax.dot_general(
        token_map, normed, (((0,), (0,)), ((), ())), preferred_element_type=jnp.float32
    ).astype(jnp.bfloat16)
    send_grads = lax.dot_general(
        weighted,
        grad_float,
        (((0,), (0,)), ((), ())),
        precision=lax.Precision.HIGHEST,
        preferred_element_type=jnp.float32,
    ).astype(jnp.bfloat16)
    rows_in, grads_in = (
        lax.all_to_all(
            send_rows.reshape(experts, slots, width),
            ("ctx", "grp"),
            split_axis=0,
            concat_axis=0,
            tiled=True,
        ),
        lax.all_to_all(
            send_grads.reshape(experts, slots, width),
            ("ctx", "grp"),
            split_axis=0,
            concat_axis=0,
            tiled=True,
        ),
    )
    full_gate, full_up, full_down = (
        lax.all_gather(w_gate[0], "side", axis=1, tiled=True),
        lax.all_gather(w_up[0], "side", axis=1, tiled=True),
        lax.all_gather(w_down[0], "side", axis=0, tiled=True),
    )
    output, d_rows, g_gate, g_up, g_down = expert_pass(
        rows_in.reshape(places, width),
        grads_in.reshape(places, width),
        full_gate,
        full_up,
        full_down,
    )
    own_gate, own_up, own_down = (
        lax.psum_scatter(g_gate, "side", scatter_dimension=1, tiled=True),
        lax.psum_scatter(g_up, "side", scatter_dimension=1, tiled=True),
        lax.psum_scatter(g_down, "side", scatter_dimension=0, tiled=True),
    )
    back_out = output.astype(jnp.bfloat16)
    back_rows = d_rows.astype(jnp.bfloat16)
    came_out, came_rows = (
        lax.all_to_all(
            back_out.reshape(experts, slots, width),
            ("ctx", "grp"),
            split_axis=0,
            concat_axis=0,
            tiled=True,
        ),
        lax.all_to_all(
            back_rows.reshape(experts, slots, width),
            ("ctx", "grp"),
            split_axis=0,
            concat_axis=0,
            tiled=True,
        ),
    )
    slot_out = jnp.dot(
        select.astype(jnp.bfloat16),
        came_out.reshape(places, width),
        preferred_element_type=jnp.float32,
    ).reshape(count, chosen, width)
    mixed = (x_float + jnp.sum(combine[:, :, None] * slot_out, axis=1)).astype(jnp.bfloat16)
    d_combine = jnp.einsum("tkd,td->tk", slot_out, grad_float, precision=lax.Precision.HIGHEST)
    d_normed = jnp.dot(
        token_map, came_rows.reshape(places, width), preferred_element_type=jnp.float32
    )
    d_gain = lax.psum(jnp.sum(d_normed * x_float * inv_rms, axis=0), ("ctx", "grp", "side"))
    scaled = d_normed * norm_gain
    d_tokens = (
        grad_float
        + inv_rms * scaled
        - x_float * inv_rms**3 * jnp.mean(scaled * x_float, axis=1, keepdims=True)
    )
    return (
        mixed,
        d_tokens.astype(jnp.bfloat16),
        d_gain,
        d_combine,
        own_gate.astype(jnp.bfloat16)[None],
        own_up.astype(jnp.bfloat16)[None],
        own_down.astype(jnp.bfloat16)[None],
    )


def solution(mesh):
    in_specs = (
        P(("ctx", "grp", "side"), None),
        P(),
        P(("ctx", "grp", "side"), None),
        P(("ctx", "grp", "side"), None),
        P(("ctx", "grp"), None, "side"),
        P(("ctx", "grp"), None, "side"),
        P(("ctx", "grp"), "side", None),
        P(("ctx", "grp", "side"), None),
    )
    out_specs = (
        P(("ctx", "grp", "side"), None),
        P(("ctx", "grp", "side"), None),
        P(),
        P(("ctx", "grp", "side"), None),
        P(("ctx", "grp"), None, "side"),
        P(("ctx", "grp"), None, "side"),
        P(("ctx", "grp"), "side", None),
    )
    return jax.shard_map(local, mesh=mesh, in_specs=in_specs, out_specs=out_specs, check_vma=False)
```

profile of v0, /device:TPU:12, one launch (start us, length us, event | category | flops | bytes accessed | tf_op | source)
XLA Modules:
  0.0 222.5 jit_solution(12201147010498002594)
XLA Ops:
  7.2 0.0 all-gather.11.cloned.1.call-start
  7.2 0.7 all-gather.11.cloned.1.call-update
  7.9 0.0 all-gather.9.cloned.1.call-start
  8.0 0.7 all-gather.9.cloned.1.call-update
  8.7 0.1 copy.23
  8.8 0.1 copy.24
  8.8 0.1 eq.49
  8.9 0.1 fusion.41
  9.0 0.2 reduce_window_sum.11
  9.2 0.2 select_reduce_fusion.1
  9.4 0.1 reduce_sum.66
  9.5 0.0 copy-start.10
  9.5 0.0 copy-start.6
  9.5 0.2 select_reduce_fusion
  9.7 0.0 copy-start.7
  9.7 0.8 convolution_convert_fusion
  10.5 1.2 reshape.111
  11.7 7.2 %all-to-all-start.2 = ((bf16[16,11,2048]{2,1,0:T(8,128)(2,1)}), bf16[16,11,2048]{2,1,0:T(8,128)(2,1)S(1)}, u32[]{:S(2)}, u32[]{:S(2)}) async-start(bf16[16,11,2048]{2,1,0:T(8,128)(2,1)} %reshape.111), calls=%async_computation.2 | async-start | bytes 2097152 | tf_op jit(solution)/shard_map/all_to_all | solution.py:79
  18.9 0.0 all-gather.7.cloned.1.call-start
  18.9 0.7 all-gather.7.cloned.1.call-update
  19.6 0.1 fusion.22
  19.8 0.5 multiply_multiply_fusion
  20.3 0.4 convolution_convert_fusion.1
  20.7 1.2 reshape.107
  21.9 20.6 %all-to-all-done.2 = bf16[16,11,2048]{2,1,0:T(8,128)(2,1)S(1)} async-done(((bf16[16,11,2048]{2,1,0:T(8,128)(2,1)}), bf16[16,11,2048]{2,1,0:T(8,128)(2,1)S(1)}, u32[]{:S(2)}, u32[]{:S(2)}) %all-to-all-start.2) | async-done | bytes 720928 | tf_op jit(solution)/shard_map/all_to_all | solution.py:79
  42.5 7.5 %all-to-all-start = ((bf16[16,11,2048]{2,1,0:T(8,128)(2,1)}), bf16[16,11,2048]{2,1,0:T(8,128)(2,1)S(1)}, u32[]{:S(2)}, u32[]{:S(2)}) async-start(bf16[16,11,2048]{2,1,0:T(8,128)(2,1)} %reshape.107), calls=%async_computation | async-start | bytes 2097152 | tf_op jit(solution)/shard_map/all_to_all | solution.py:72
  49.9 0.0 reduce-scatter.8.cloned.1.call-start
  50.0 0.3 reshape.112
  50.3 22.6 %all-to-all-done = bf16[16,11,2048]{2,1,0:T(8,128)(2,1)S(1)} async-done(((bf16[16,11,2048]{2,1,0:T(8,128)(2,1)}), bf16[16,11,2048]{2,1,0:T(8,128)(2,1)S(1)}, u32[]{:S(2)}, u32[]{:S(2)}) %all-to-all-start) | async-done | bytes 720928 | tf_op jit(solution)/shard_map/all_to_all | solution.py:72
  72.9 0.3 reshape.108
  73.2 0.0 all-gather.11.cloned.1.call-done
  73.2 3.1 %fusion = f32[176,768]{1,0:T(8,128)S(1)} fusion(bf16[176,2048]{1,0:T(8,128)(2,1)S(1)} %reshape.112, bf16[1,768,2048]{2,1,0:T(8,128)(2,1)} %all-gather.11.cloned.1.call-done), kind=kOutput, calls=%fused_computation | convolution fusion | flops 553648128 | bytes 4407296 | tf_op jit(solution)/shard_map/dot_general | solution.py:16
  76.3 0.0 all-gather.9.cloned.1.call-done
  76.4 2.6 %fusion.6 = f32[176,768]{1,0:T(8,128)S(1)} fusion(bf16[176,2048]{1,0:T(8,128)(2,1)S(1)} %reshape.108, bf16[1,2048,768]{2,1,0:T(8,128)(2,1)} %all-gather.9.cloned.1.call-done), kind=kOutput, calls=%fused_computation.6 | convolution fusion | flops 553648128 | bytes 4407296 | tf_op jit(solution)/shard_map/dot_general | solution.py:11
  79.0 0.0 all-gather.7.cloned.1.call-done
  79.0 2.8 %multiply_convert_fusion.1 = (bf16[176,768]{1,0:T(8,128)(2,1)S(1)}, bf16[176,768]{1,0:T(8,128)(2,1)S(1)}, bf16[176,768]{1,0:T(8,128)(2,1)S(1)}) fusion(f32[176,768]{1,0:T(8,128)S(1)} %fusion, f32[176,768]{1,0:T(8,128)S(1)} %fusion.6, bf16[176,2048]{1,0:T(8,128)(2,1)S(1)} %reshape.108, bf16[1,2048,768]{2,1,0:T(8,128)(2,1)} %all-gather.7.cloned.1.call-done), kind=kOutput, calls=%fused_computation.22 | convolution fusion | flops 555675648 | bytes 5758976 | tf_op jit(solution)/shard_map/dot_general | solution.py:10
  81.8 3.6 %fusion.47 = f32[768,2048]{1,0:T(8,128)} fusion(bf16[176,768]{1,0:T(8,128)(2,1)S(1)} %get-tuple-element.13, bf16[176,2048]{1,0:T(8,128)(2,1)S(1)} %reshape.112), kind=kOutput, calls=%fused_computation.66 | convolution fusion | flops 553648128 | bytes 7282688 | tf_op jit(solution)/shard_map/dot_general | solution.py:33
  85.5 0.0 reduce-scatter.8.cloned.1.call-update
  85.5 0.0 reduce-scatter.4.cloned.1.call-start
  85.5 3.7 %fusion.45 = f32[2048,768]{1,0:T(8,128)} fusion(bf16[176,2048]{1,0:T(8,128)(2,1)S(1)} %reshape.108, bf16[176,768]{1,0:T(8,128)(2,1)S(1)} %get-tuple-element.11), kind=kOutput, calls=%fused_computation.64 | convolution fusion | flops 553648128 | bytes 7282688 | tf_op jit(solution)/shard_map/dot_general | solution.py:29
  89.2 0.0 reduce-scatter.4.cloned.1.call-update
  89.3 0.0 reduce-scatter.6.cloned.1.call-start
  89.3 4.0 %fusion.46 = f32[2048,768]{1,0:T(8,128)} fusion(bf16[176,2048]{1,0:T(8,128)(2,1)S(1)} %reshape.108, bf16[176,768]{1,0:T(8,128)(2,1)S(1)} %get-tuple-element.12), kind=kOutput, calls=%fused_computation.65 | convolution fusion | flops 553648128 | bytes 7282688 | tf_op jit(solution)/shard_map/dot_general | solution.py:32
  93.3 0.0 reduce-scatter.6.cloned.1.call-update
  93.4 3.7 %fusion.15 = bf16[176,2048]{1,0:T(8,128)(2,1)} fusion(bf16[176,768]{1,0:T(8,128)(2,1)S(1)} %get-tuple-element.13, bf16[1,768,2048]{2,1,0:T(8,128)(2,1)} %all-gather.11.cloned.1.call-done), kind=kOutput, calls=%fused_computation.13 | convolution fusion | flops 554008576 | bytes 4136960 | tf_op jit(solution)/shard_map/dot_general | solution.py:15
  97.1 2.6 %reshape.109 = bf16[16,11,2048]{2,1,0:T(8,128)(2,1)} reshape(bf16[176,2048]{1,0:T(8,128)(2,1)} %fusion.15) | data formatting | bytes 1441792 | tf_op jit(solution)/shard_map/reshape | solution.py:108
  99.6 9.3 %all-to-all-start.1 = ((bf16[16,11,2048]{2,1,0:T(8,128)(2,1)}), bf16[16,11,2048]{2,1,0:T(8,128)(2,1)}, u32[]{:S(2)}, u32[]{:S(2)}) async-start(bf16[16,11,2048]{2,1,0:T(8,128)(2,1)} %reshape.109), calls=%async_computation.1 | async-start | bytes 2097152 | tf_op jit(solution)/shard_map/all_to_all | solution.py:107
  108.9 2.3 %fusion.4 = f32[176,2048]{1,0:T(8,128)S(1)} fusion(bf16[176,768]{1,0:T(8,128)(2,1)} %copy-done.4, bf16[1,2048,768]{2,1,0:T(8,128)(2,1)S(1)} %copy-done), kind=kOutput, calls=%fused_computation.4 | convolution fusion | flops 553648128 | bytes 4857856 | tf_op jit(solution)/shard_map/dot_general | solution.py:26
  111.2 1.2 fusion.18
  112.4 1.2 reshape.113
  113.7 17.7 %all-to-all-done.1 = bf16[16,11,2048]{2,1,0:T(8,128)(2,1)} async-done(((bf16[16,11,2048]{2,1,0:T(8,128)(2,1)}), bf16[16,11,2048]{2,1,0:T(8,128)(2,1)}, u32[]{:S(2)}, u32[]{:S(2)}) %all-to-all-start.1) | async-done | bytes 720928 | tf_op jit(solution)/shard_map/all_to_all | solution.py:107
  131.4 7.5 %all-to-all-start.3 = ((bf16[16,11,2048]{2,1,0:T(8,128)(2,1)}), bf16[16,11,2048]{2,1,0:T(8,128)(2,1)S(1)}, u32[]{:S(2)}, u32[]{:S(2)}) async-start(bf16[16,11,2048]{2,1,0:T(8,128)(2,1)} %reshape.113), calls=%async_computation.3 | async-start | bytes 2097152 | tf_op jit(solution)/shard_map/all_to_all | solution.py:114
  138.9 1.5 reshape.118
  140.4 0.5 multiply_reduce_fusion
  140.9 1.1 fusion.32
  142.1 0.7 copy.28
  142.8 19.0 %all-to-all-done.3 = bf16[16,11,2048]{2,1,0:T(8,128)(2,1)S(1)} async-done(((bf16[16,11,2048]{2,1,0:T(8,128)(2,1)}), bf16[16,11,2048]{2,1,0:T(8,128)(2,1)S(1)}, u32[]{:S(2)}, u32[]{:S(2)}) %all-to-all-start.3) | async-done | bytes 720928 | tf_op jit(solution)/shard_map/all_to_all | solution.py:114
  161.8 0.3 reshape.114
  162.1 0.3 fusion.31
  162.4 42.8 %psum.7 = f32[2048]{0:T(1024)} all-reduce(f32[2048]{0:T(1024)S(1)} %get-tuple-element.7), channel_id=1, replica_groups=mesh['ctx'=4,'grp'=4,'side'=2] {'ctx','grp','side'}, use_global_device_ids=true, to_apply=%region_8.9 | all-reduce | flops 2048 | bytes 16384 | tf_op jit(solution)/shard_map/psum | solution.py:132
  205.2 0.7 fusion.28
  206.0 3.3 %convert_bitcast_fusion = bf16[1,384,2048]{2,1,0:T(8,128)(2,1)} fusion(f32[384,2048]{1,0:T(8,128)} %reduce-scatter.8.cloned.1.call-done), kind=kLoop, calls=%fused_computation.17 | loop fusion | flops 786432 | bytes 4718592 | tf_op jit(solution)/shard_map/broadcast_in_dim | solution.py:146
  209.2 3.2 %convert_bitcast_fusion.2 = bf16[1,2048,384]{2,1,0:T(8,128)(2,1)} fusion(f32[2048,384]{1,0:T(8,128)} %reduce-scatter.4.cloned.1.call-done), kind=kLoop, calls=%fused_computation.19 | loop fusion | flops 786432 | bytes 4718592 | tf_op jit(solution)/shard_map/broadcast_in_dim | solution.py:144
  212.4 3.2 %convert_bitcast_fusion.1 = bf16[1,2048,384]{2,1,0:T(8,128)(2,1)} fusion(f32[2048,384]{1,0:T(8,128)} %reduce-scatter.6.cloned.1.call-done), kind=kLoop, calls=%fused_computation.18 | loop fusion | flops 786432 | bytes 4718592 | tf_op jit(solution)/shard_map/broadcast_in_dim | solution.py:145
  (40 shorter events, 0.1 us)
Async XLA Ops:
  7.2 1.5 copy-start.16
  7.2 1.6 copy-start.17
  7.2 2.5 %copy-start.5 = (bf16[16,2048]{1,0:T(8,128)(2,1)S(1)}, bf16[16,2048]{1,0:T(8,128)(2,1)}, u32[]{:S(2)}) copy-start(bf16[16,2048]{1,0:T(8,128)(2,1)} %param.15) | copy-start | bytes 196612
  7.2 66.0 %all-gather.11.cloned.1.call-start = ((), (), s32[]{:S(2)}) async-start(), calls=%async_computation.12 | async-start | bytes 4718592 | tf_op jit(solution)/shard_map/all_gather | solution.py:90
  7.9 68.4 %all-gather.9.cloned.1.call-start = ((), (), s32[]{:S(2)}) async-start(), calls=%async_computation.11 | async-start | bytes 4718592 | tf_op jit(solution)/shard_map/all_gather | solution.py:89
  8.8 10.8 %copy-start.12 = (f32[16,8]{1,0:T(8,128)}, f32[16,8]{1,0:T(8,128)S(1)}, u32[]{:S(2)}) copy-start(f32[16,8]{1,0:T(8,128)S(1)} %copy.23) | copy-start | bytes 1540
  9.5 10.3 %copy-start.10 = (s32[16,8]{1,0:T(8,128)}, s32[16,8]{1,0:T(8,128)S(1)}, u32[]{:S(2)}) copy-start(s32[16,8]{1,0:T(8,128)S(1)} %multiply_add_fusion) | copy-start | bytes 1540
  9.5 10.1 %copy-start.6 = (bf16[16,2048]{1,0:T(8,128)(2,1)S(1)}, bf16[16,2048]{1,0:T(8,128)(2,1)}, u32[]{:S(2)}) copy-start(bf16[16,2048]{1,0:T(8,128)(2,1)} %param.8) | copy-start | bytes 196612
  9.7 10.6 %copy-start.8 = (bf16[16,176]{1,0:T(8,128)(2,1)}, bf16[16,176]{1,0:T(8,128)(2,1)S(1)}, u32[]{:S(2)}) copy-start(bf16[16,176]{1,0:T(8,128)(2,1)S(1)} %get-tuple-element.10) | copy-start | bytes 16900
  9.7 10.6 %copy-start.7 = (f32[2048]{0:T(1024)S(1)}, f32[2048]{0:T(1024)}, u32[]{:S(2)}) copy-start(f32[2048]{0:T(1024)} %param.9) | copy-start | bytes 24580
  11.7 30.8 %all-to-all-start.2 = ((bf16[16,11,2048]{2,1,0:T(8,128)(2,1)}), bf16[16,11,2048]{2,1,0:T(8,128)(2,1)S(1)}, u32[]{:S(2)}, u32[]{:S(2)}) async-start(bf16[16,11,2048]{2,1,0:T(8,128)(2,1)} %reshape.111), calls=%async_computation.2 | async-start | bytes 2097152 | tf_op jit(solution)/shard_map/all_to_all | solution.py:79
  18.9 60.1 %all-gather.7.cloned.1.call-start = ((), (), s32[]{:S(2)}) async-start(), calls=%async_computation.10 | async-start | bytes 4718592 | tf_op jit(solution)/shard_map/all_gather | solution.py:88
  20.3 22.2 %copy-start.14 = (f32[16]{0:T(128)}, f32[16]{0:T(128)S(1)}, u32[]{:S(2)}) copy-start(f32[16]{0:T(128)S(1)} %get-tuple-element.17) | copy-start | bytes 196
  42.5 30.5 %all-to-all-start = ((bf16[16,11,2048]{2,1,0:T(8,128)(2,1)}), bf16[16,11,2048]{2,1,0:T(8,128)(2,1)S(1)}, u32[]{:S(2)}, u32[]{:S(2)}) async-start(bf16[16,11,2048]{2,1,0:T(8,128)(2,1)} %reshape.107), calls=%async_computation | async-start | bytes 2097152 | tf_op jit(solution)/shard_map/all_to_all | solution.py:72
  49.9 156.0 %reduce-scatter.8.cloned.1.call-start = ((), (), s32[]{:S(2)}) async-start(), calls=%async_computation.9 | async-start | bytes 9437184 | tf_op jit(solution)/shard_map/reduce_scatter | solution.py:102
  81.8 3.7 %copy-start.2 = (bf16[176,768]{1,0:T(8,128)(2,1)}, bf16[176,768]{1,0:T(8,128)(2,1)S(1)}, u32[]{:S(2)}) copy-start(bf16[176,768]{1,0:T(8,128)(2,1)S(1)} %get-tuple-element.11) | copy-start | bytes 811012
  81.8 7.5 %copy-start.4 = (bf16[176,768]{1,0:T(8,128)(2,1)}, bf16[176,768]{1,0:T(8,128)(2,1)S(1)}, u32[]{:S(2)}) copy-start(bf16[176,768]{1,0:T(8,128)(2,1)S(1)} %get-tuple-element.12) | copy-start | bytes 811012
  85.5 123.8 %reduce-scatter.4.cloned.1.call-start = ((), (), s32[]{:S(2)}) async-start(), calls=%async_computation.7 | async-start | bytes 9437184 | tf_op jit(solution)/shard_map/reduce_scatter | solution.py:100
  89.3 123.2 %reduce-scatter.6.cloned.1.call-start = ((), (), s32[]{:S(2)}) async-start(), calls=%async_computation.8 | async-start | bytes 9437184 | tf_op jit(solution)/shard_map/reduce_scatter | solution.py:101
  93.3 15.6 %copy-start = (bf16[1,2048,768]{2,1,0:T(8,128)(2,1)S(1)}, bf16[1,2048,768]{2,1,0:T(8,128)(2,1)}, u32[]{:S(2)}) copy-start(bf16[1,2048,768]{2,1,0:T(8,128)(2,1)} %all-gather.9.cloned.1.call-done) | copy-start | bytes 9437188
  99.6 11.6 %copy-start.3 = (bf16[176,768]{1,0:T(8,128)(2,1)S(1)}, bf16[176,768]{1,0:T(8,128)(2,1)}, u32[]{:S(2)}) copy-start(bf16[176,768]{1,0:T(8,128)(2,1)} %copy-done.2) | copy-start | bytes 811012
  99.6 31.8 %all-to-all-start.1 = ((bf16[16,11,2048]{2,1,0:T(8,128)(2,1)}), bf16[16,11,2048]{2,1,0:T(8,128)(2,1)}, u32[]{:S(2)}, u32[]{:S(2)}) async-start(bf16[16,11,2048]{2,1,0:T(8,128)(2,1)} %reshape.109), calls=%async_computation.1 | async-start | bytes 2097152 | tf_op jit(solution)/shard_map/all_to_all | solution.py:107
  108.9 2.3 %copy-start.1 = (bf16[1,2048,768]{2,1,0:T(8,128)(2,1)S(1)}, bf16[1,2048,768]{2,1,0:T(8,128)(2,1)}, u32[]{:S(2)}) copy-start(bf16[1,2048,768]{2,1,0:T(8,128)(2,1)} %all-gather.7.cloned.1.call-done) | copy-start | bytes 9437188
  112.4 28.0 %copy-start.11 = (s32[16,8]{1,0:T(8,128)S(1)}, s32[16,8]{1,0:T(8,128)}, u32[]{:S(2)}) copy-start(s32[16,8]{1,0:T(8,128)} %copy-done.10) | copy-start | bytes 1540
  112.4 28.0 %copy-start.13 = (f32[16,8]{1,0:T(8,128)S(1)}, f32[16,8]{1,0:T(8,128)}, u32[]{:S(2)}) copy-start(f32[16,8]{1,0:T(8,128)} %copy-done.12) | copy-start | bytes 1540
  131.4 30.4 %all-to-all-start.3 = ((bf16[16,11,2048]{2,1,0:T(8,128)(2,1)}), bf16[16,11,2048]{2,1,0:T(8,128)(2,1)S(1)}, u32[]{:S(2)}, u32[]{:S(2)}) async-start(bf16[16,11,2048]{2,1,0:T(8,128)(2,1)} %reshape.113), calls=%async_computation.3 | async-start | bytes 2097152 | tf_op jit(solution)/shard_map/all_to_all | solution.py:114
  138.9 23.2 %copy-start.9 = (bf16[16,176]{1,0:T(8,128)(2,1)S(1)}, bf16[16,176]{1,0:T(8,128)(2,1)}, u32[]{:S(2)}) copy-start(bf16[16,176]{1,0:T(8,128)(2,1)} %copy-done.8) | copy-start | bytes 16900
  138.9 23.2 %copy-start.15 = (f32[16]{0:T(128)S(1)}, f32[16]{0:T(128)}, u32[]{:S(2)}) copy-start(f32[16]{0:T(128)} %copy-done.14) | copy-start | bytes 196
  140.4 64.8 %copy-start.18 = (f32[16]{0:T(128)S(1)}, f32[16]{0:T(128)}, u32[]{:S(2)}) copy-start(f32[16]{0:T(128)} %get-tuple-element.16) | copy-start | bytes 196
Sparse Core Ops, SparseCore 0:
  9.6 13.4 all-gather.10
  24.6 13.1 all-gather.8
  39.4 13.1 all-gather.6
  85.6 15.8 reduce-scatter.7
  103.6 15.1 reduce-scatter.3
  120.9 15.0 reduce-scatter.5
where the time goes:
time: 223 us; the launch traced here: 222 us
  waiting for transfers between devices  82.1 us (37%)
  blocking collectives  42.8 us (19%)
  starting transfers between devices  31.6 us (14%)
  matrix products  30.1 us (13%)
  between operations  14.5 us (7%)
  other arithmetic  11.7 us (5%)
  local copies, waits for them, and re-layouts  9.69 us (4%)
    psum x1, blocking collectives, local(): lax.psum(jnp.sum(d_normed * x_float * inv_rms, axis=0), ('ctx', 'grp', 's...  42.8 us
    all_to_all x1, waiting for transfers between devices, local(): lax.all_to_all(send_rows.reshape(experts, slots, width), ('ctx', 'grp'),...  22.6 us
    all_to_all x1, waiting for transfers between devices, local(): lax.all_to_all(send_grads.reshape(experts, slots, width), ('ctx', 'grp'),...  20.6 us
    all_to_all x1, waiting for transfers between devices, local(): lax.all_to_all(back_rows.reshape(experts, slots, width), ('ctx', 'grp'),...  19 us
    all_to_all x1, waiting for transfers between devices, local(): lax.all_to_all(back_out.reshape(experts, slots, width), ('ctx', 'grp'), s...  17.7 us
    all_to_all x1, starting transfers between devices, local(): lax.all_to_all(back_out.reshape(experts, slots, width), ('ctx', 'grp'), s...  9.28 us
    all_to_all x1, starting transfers between devices, local(): lax.all_to_all(back_rows.reshape(experts, slots, width), ('ctx', 'grp'),...  7.49 us
    all_to_all x1, starting transfers between devices, local(): lax.all_to_all(send_rows.reshape(experts, slots, width), ('ctx', 'grp'),...  7.48 us
  transfers between devices with their start and end apart: 10, of which 4 were waited for; matrix products, arithmetic and copies ran while one was open for 19% of the time, Pallas kernels for 0%

commit v1 on v0

--- a/solution.py
+++ b/solution.py
@@ -129,7 +129,9 @@
     d_normed = jnp.dot(
         token_map, came_rows.reshape(places, width), preferred_element_type=jnp.float32
     )
-    d_gain = lax.psum(jnp.sum(d_normed * x_float * inv_rms, axis=0), ("ctx", "grp", "side"))
+    d_gain = lax.psum(
+        lax.psum(jnp.sum(d_normed * x_float * inv_rms, axis=0), ("grp", "side")), "ctx"
+    )
     scaled = d_normed * norm_gain
     d_tokens = (
         grad_float

time: 223 us -> 209 us (0.937)
  the two profiles are of different devices: /device:TPU:12 before, /device:TPU:0 now
where the time goes in v1:
time: 209 us; the launch traced here: 208 us
  waiting for transfers between devices  97.1 us (46%)
  matrix products  31.4 us (15%)
  blocking collectives  23.7 us (11%)
  starting transfers between devices  20.6 us (10%)
  between operations  14.5 us (7%)
  other arithmetic  11.7 us (6%)
  local copies, waits for them, and re-layouts  9.45 us (5%)
    all_to_all x1, waiting for transfers between devices, local(): lax.all_to_all(send_rows.reshape(experts, slots, width), ('ctx', 'grp'),...  26.4 us
    all_to_all x1, waiting for transfers between devices, local(): lax.all_to_all(send_grads.reshape(experts, slots, width), ('ctx', 'grp'),...  24.4 us
    all_to_all x1, waiting for transfers between devices, local(): lax.all_to_all(back_rows.reshape(experts, slots, width), ('ctx', 'grp'),...  22.6 us
    all_to_all x1, waiting for transfers between devices, local(): lax.all_to_all(back_out.reshape(experts, slots, width), ('ctx', 'grp'), s...  21.5 us
    psum x1, blocking collectives, local(): lax.psum(jnp.sum(d_normed * x_float * inv_rms, axis=0), ('grp', 'side'))  13.9 us
    psum x1, blocking collectives, local(): lax.psum(lax.psum(jnp.sum(d_normed * x_float * inv_rms, axis=0), ('grp',...  9.75 us
    all_to_all x1, starting transfers between devices, local(): lax.all_to_all(send_grads.reshape(experts, slots, width), ('ctx', 'grp'),...  8.34 us
    dot_general x1, matrix products, expert_pass(): lax.dot_general(rows, d_up, (((0,), (0,)), ((), ())), preferred_element_t...  4.81 us
  transfers between devices with their start and end apart: 10, of which 4 were waited for; matrix products, arithmetic and copies ran while one was open for 21% of the time, Pallas kernels for 0%

profile of v1, /device:TPU:0, one launch (start us, length us, event | category | flops | bytes accessed | tf_op | source)
XLA Modules:
  0.0 208.4 jit_solution(7806166026354713469)
XLA Ops:
  7.2 0.0 all-gather.11.cloned.1.call-start
  7.2 0.7 all-gather.11.cloned.1.call-update
  7.9 0.0 all-gather.9.cloned.1.call-start
  8.0 0.7 all-gather.9.cloned.1.call-update
  8.7 0.1 copy.23
  8.8 0.1 copy.24
  8.8 0.1 eq.49
  8.9 0.1 fusion.41
  9.0 0.2 reduce_window_sum.11
  9.2 0.2 select_reduce_fusion.1
  9.4 0.1 reduce_sum.66
  9.5 0.0 copy-start.10
  9.5 0.2 select_reduce_fusion
  9.7 0.0 copy-start.7
  9.7 0.8 convolution_convert_fusion
  10.5 1.2 reshape.111
  11.7 8.3 %all-to-all-start.2 = ((bf16[16,11,2048]{2,1,0:T(8,128)(2,1)}), bf16[16,11,2048]{2,1,0:T(8,128)(2,1)S(1)}, u32[]{:S(2)}, u32[]{:S(2)}) async-start(bf16[16,11,2048]{2,1,0:T(8,128)(2,1)} %reshape.111), calls=%async_computation.2 | async-start | bytes 2097152 | tf_op jit(solution)/shard_map/all_to_all | solution.py:79
  20.0 0.0 all-gather.7.cloned.1.call-start
  20.1 0.7 all-gather.7.cloned.1.call-update
  20.8 0.1 fusion.22
  20.9 0.6 multiply_multiply_fusion
  21.5 0.4 convolution_convert_fusion.1
  21.9 1.2 reshape.107
  23.2 24.4 %all-to-all-done.2 = bf16[16,11,2048]{2,1,0:T(8,128)(2,1)S(1)} async-done(((bf16[16,11,2048]{2,1,0:T(8,128)(2,1)}), bf16[16,11,2048]{2,1,0:T(8,128)(2,1)S(1)}, u32[]{:S(2)}, u32[]{:S(2)}) %all-to-all-start.2) | async-done | bytes 720928 | tf_op jit(solution)/shard_map/all_to_all | solution.py:79
  47.5 3.7 %all-to-all-start = ((bf16[16,11,2048]{2,1,0:T(8,128)(2,1)}), bf16[16,11,2048]{2,1,0:T(8,128)(2,1)S(1)}, u32[]{:S(2)}, u32[]{:S(2)}) async-start(bf16[16,11,2048]{2,1,0:T(8,128)(2,1)} %reshape.107), calls=%async_computation | async-start | bytes 2097152 | tf_op jit(solution)/shard_map/all_to_all | solution.py:72
  51.2 0.0 reduce-scatter.8.cloned.1.call-start
  51.2 0.3 reshape.112
  51.5 26.4 %all-to-all-done = bf16[16,11,2048]{2,1,0:T(8,128)(2,1)S(1)} async-done(((bf16[16,11,2048]{2,1,0:T(8,128)(2,1)}), bf16[16,11,2048]{2,1,0:T(8,128)(2,1)S(1)}, u32[]{:S(2)}, u32[]{:S(2)}) %all-to-all-start) | async-done | bytes 720928 | tf_op jit(solution)/shard_map/all_to_all | solution.py:72
  78.0 0.3 reshape.108
  78.3 0.0 all-gather.11.cloned.1.call-done
  78.3 3.1 %fusion = f32[176,768]{1,0:T(8,128)S(1)} fusion(bf16[176,2048]{1,0:T(8,128)(2,1)S(1)} %reshape.112, bf16[1,768,2048]{2,1,0:T(8,128)(2,1)} %all-gather.11.cloned.1.call-done), kind=kOutput, calls=%fused_computation | convolution fusion | flops 553648128 | bytes 4407296 | tf_op jit(solution)/shard_map/dot_general | solution.py:16
  81.4 0.0 all-gather.9.cloned.1.call-done
  81.4 2.6 %fusion.6 = f32[176,768]{1,0:T(8,128)S(1)} fusion(bf16[176,2048]{1,0:T(8,128)(2,1)S(1)} %reshape.108, bf16[1,2048,768]{2,1,0:T(8,128)(2,1)} %all-gather.9.cloned.1.call-done), kind=kOutput, calls=%fused_computation.6 | convolution fusion | flops 553648128 | bytes 4407296 | tf_op jit(solution)/shard_map/dot_general | solution.py:11
  84.0 0.0 all-gather.7.cloned.1.call-done
  84.1 2.8 %multiply_convert_fusion.1 = (bf16[176,768]{1,0:T(8,128)(2,1)S(1)}, bf16[176,768]{1,0:T(8,128)(2,1)S(1)}, bf16[176,768]{1,0:T(8,128)(2,1)S(1)}) fusion(f32[176,768]{1,0:T(8,128)S(1)} %fusion, f32[176,768]{1,0:T(8,128)S(1)} %fusion.6, bf16[176,2048]{1,0:T(8,128)(2,1)S(1)} %reshape.108, bf16[1,2048,768]{2,1,0:T(8,128)(2,1)} %all-gather.7.cloned.1.call-done), kind=kOutput, calls=%fused_computation.22 | convolution fusion | flops 555675648 | bytes 5758976 | tf_op jit(solution)/shard_map/dot_general | solution.py:10
  86.9 3.6 %fusion.47 = f32[768,2048]{1,0:T(8,128)} fusion(bf16[176,768]{1,0:T(8,128)(2,1)S(1)} %get-tuple-element.13, bf16[176,2048]{1,0:T(8,128)(2,1)S(1)} %reshape.112), kind=kOutput, calls=%fused_computation.66 | convolution fusion | flops 553648128 | bytes 7282688 | tf_op jit(solution)/shard_map/dot_general | solution.py:33
  90.5 0.0 reduce-scatter.8.cloned.1.call-update
  90.5 0.0 reduce-scatter.4.cloned.1.call-start
  90.6 4.0 %fusion.45 = f32[2048,768]{1,0:T(8,128)} fusion(bf16[176,2048]{1,0:T(8,128)(2,1)S(1)} %reshape.108, bf16[176,768]{1,0:T(8,128)(2,1)S(1)} %get-tuple-element.11), kind=kOutput, calls=%fused_computation.64 | convolution fusion | flops 553648128 | bytes 7282688 | tf_op jit(solution)/shard_map/dot_general | solution.py:29
  94.6 0.0 reduce-scatter.4.cloned.1.call-update
  94.6 0.0 reduce-scatter.6.cloned.1.call-start
  94.7 4.8 %fusion.46 = f32[2048,768]{1,0:T(8,128)} fusion(bf16[176,2048]{1,0:T(8,128)(2,1)S(1)} %reshape.108, bf16[176,768]{1,0:T(8,128)(2,1)S(1)} %get-tuple-element.12), kind=kOutput, calls=%fused_computation.65 | convolution fusion | flops 553648128 | bytes 7282688 | tf_op jit(solution)/shard_map/dot_general | solution.py:32
  99.5 0.0 reduce-scatter.6.cloned.1.call-update
  99.5 3.9 %fusion.15 = bf16[176,2048]{1,0:T(8,128)(2,1)} fusion(bf16[176,768]{1,0:T(8,128)(2,1)S(1)} %get-tuple-element.13, bf16[1,768,2048]{2,1,0:T(8,128)(2,1)} %all-gather.11.cloned.1.call-done), kind=kOutput, calls=%fused_computation.13 | convolution fusion | flops 554008576 | bytes 4136960 | tf_op jit(solution)/shard_map/dot_general | solution.py:15
  103.4 2.3 %reshape.109 = bf16[16,11,2048]{2,1,0:T(8,128)(2,1)} reshape(bf16[176,2048]{1,0:T(8,128)(2,1)} %fusion.15) | data formatting | bytes 1441792 | tf_op jit(solution)/shard_map/reshape | solution.py:108
  105.7 4.5 %all-to-all-start.1 = ((bf16[16,11,2048]{2,1,0:T(8,128)(2,1)}), bf16[16,11,2048]{2,1,0:T(8,128)(2,1)}, u32[]{:S(2)}, u32[]{:S(2)}) async-start(bf16[16,11,2048]{2,1,0:T(8,128)(2,1)} %reshape.109), calls=%async_computation.1 | async-start | bytes 2097152 | tf_op jit(solution)/shard_map/all_to_all | solution.py:107
  110.2 2.3 %fusion.4 = f32[176,2048]{1,0:T(8,128)S(1)} fusion(bf16[176,768]{1,0:T(8,128)(2,1)} %copy-done.4, bf16[1,2048,768]{2,1,0:T(8,128)(2,1)S(1)} %copy-done), kind=kOutput, calls=%fused_computation.4 | convolution fusion | flops 553648128 | bytes 4857856 | tf_op jit(solution)/shard_map/dot_general | solution.py:26
  112.5 1.2 fusion.18
  113.7 1.2 reshape.113
  115.0 21.5 %all-to-all-done.1 = bf16[16,11,2048]{2,1,0:T(8,128)(2,1)} async-done(((bf16[16,11,2048]{2,1,0:T(8,128)(2,1)}), bf16[16,11,2048]{2,1,0:T(8,128)(2,1)}, u32[]{:S(2)}, u32[]{:S(2)}) %all-to-all-start.1) | async-done | bytes 720928 | tf_op jit(solution)/shard_map/all_to_all | solution.py:107
  136.4 3.8 %all-to-all-start.3 = ((bf16[16,11,2048]{2,1,0:T(8,128)(2,1)}), bf16[16,11,2048]{2,1,0:T(8,128)(2,1)S(1)}, u32[]{:S(2)}, u32[]{:S(2)}) async-start(bf16[16,11,2048]{2,1,0:T(8,128)(2,1)} %reshape.113), calls=%async_computation.3 | async-start | bytes 2097152 | tf_op jit(solution)/shard_map/all_to_all | solution.py:114
  140.3 1.5 reshape.118
  141.8 0.5 multiply_reduce_fusion
  142.3 1.1 fusion.32
  143.5 0.7 copy.28
  144.2 22.6 %all-to-all-done.3 = bf16[16,11,2048]{2,1,0:T(8,128)(2,1)S(1)} async-done(((bf16[16,11,2048]{2,1,0:T(8,128)(2,1)}), bf16[16,11,2048]{2,1,0:T(8,128)(2,1)S(1)}, u32[]{:S(2)}, u32[]{:S(2)}) %all-to-all-start.3) | async-done | bytes 720928 | tf_op jit(solution)/shard_map/all_to_all | solution.py:114
  166.8 0.3 reshape.114
  167.1 0.3 fusion.31
  167.4 13.9 %psum.14 = f32[2048]{0:T(1024)S(1)} all-reduce(f32[2048]{0:T(1024)S(1)} %get-tuple-element.7), channel_id=1, replica_groups=mesh['ctx'=4,'grp'=4,'side'=2] {'grp','side'}, use_global_device_ids=true, to_apply=%region_8.9 | all-reduce | flops 2048 | bytes 16384 | tf_op jit(solution)/shard_map/psum | solution.py:133
  181.4 9.8 %psum.15 = f32[2048]{0:T(1024)} all-reduce(f32[2048]{0:T(1024)S(1)} %psum.14), channel_id=1, replica_groups=mesh['ctx'=4,'grp'=4,'side'=2] {'ctx'}, use_global_device_ids=true, to_apply=%region_9.10 | all-reduce | flops 2048 | bytes 16384 | tf_op jit(solution)/shard_map/psum | solution.py:132
  191.1 0.7 fusion.28
  191.8 3.3 %convert_bitcast_fusion = bf16[1,384,2048]{2,1,0:T(8,128)(2,1)} fusion(f32[384,2048]{1,0:T(8,128)} %reduce-scatter.8.cloned.1.call-done), kind=kLoop, calls=%fused_computation.17 | loop fusion | flops 786432 | bytes 4718592 | tf_op jit(solution)/shard_map/broadcast_in_dim | solution.py:148
  195.1 3.2 %convert_bitcast_fusion.2 = bf16[1,2048,384]{2,1,0:T(8,128)(2,1)} fusion(f32[2048,384]{1,0:T(8,128)} %reduce-scatter.4.cloned.1.call-done), kind=kLoop, calls=%fused_computation.19 | loop fusion | flops 786432 | bytes 4718592 | tf_op jit(solution)/shard_map/broadcast_in_dim | solution.py:146
  198.3 3.2 %convert_bitcast_fusion.1 = bf16[1,2048,384]{2,1,0:T(8,128)(2,1)} fusion(f32[2048,384]{1,0:T(8,128)} %reduce-scatter.6.cloned.1.call-done), kind=kLoop, calls=%fused_computation.18 | loop fusion | flops 786432 | bytes 4718592 | tf_op jit(solution)/shard_map/broadcast_in_dim | solution.py:147
  (41 shorter events, 0.1 us)
Async XLA Ops:
  7.2 1.5 copy-start.16
  7.2 1.6 copy-start.17
  7.2 2.5 %copy-start.5 = (bf16[16,2048]{1,0:T(8,128)(2,1)S(1)}, bf16[16,2048]{1,0:T(8,128)(2,1)}, u32[]{:S(2)}) copy-start(bf16[16,2048]{1,0:T(8,128)(2,1)} %param.15) | copy-start | bytes 196612
  7.2 71.1 %all-gather.11.cloned.1.call-start = ((), (), s32[]{:S(2)}) async-start(), calls=%async_computation.12 | async-start | bytes 4718592 | tf_op jit(solution)/shard_map/all_gather | solution.py:90
  7.9 73.5 %all-gather.9.cloned.1.call-start = ((), (), s32[]{:S(2)}) async-start(), calls=%async_computation.11 | async-start | bytes 4718592 | tf_op jit(solution)/shard_map/all_gather | solution.py:89
  8.8 12.0 %copy-start.12 = (f32[16,8]{1,0:T(8,128)}, f32[16,8]{1,0:T(8,128)S(1)}, u32[]{:S(2)}) copy-start(f32[16,8]{1,0:T(8,128)S(1)} %copy.23) | copy-start | bytes 1540
  9.5 11.5 %copy-start.10 = (s32[16,8]{1,0:T(8,128)}, s32[16,8]{1,0:T(8,128)S(1)}, u32[]{:S(2)}) copy-start(s32[16,8]{1,0:T(8,128)S(1)} %multiply_add_fusion) | copy-start | bytes 1540
  9.5 11.3 %copy-start.6 = (bf16[16,2048]{1,0:T(8,128)(2,1)S(1)}, bf16[16,2048]{1,0:T(8,128)(2,1)}, u32[]{:S(2)}) copy-start(bf16[16,2048]{1,0:T(8,128)(2,1)} %param.8) | copy-start | bytes 196612
  9.7 11.9 %copy-start.8 = (bf16[16,176]{1,0:T(8,128)(2,1)}, bf16[16,176]{1,0:T(8,128)(2,1)S(1)}, u32[]{:S(2)}) copy-start(bf16[16,176]{1,0:T(8,128)(2,1)S(1)} %get-tuple-element.10) | copy-start | bytes 16900
  9.7 11.8 %copy-start.7 = (f32[2048]{0:T(1024)S(1)}, f32[2048]{0:T(1024)}, u32[]{:S(2)}) copy-start(f32[2048]{0:T(1024)} %param.9) | copy-start | bytes 24580
  11.7 35.8 %all-to-all-start.2 = ((bf16[16,11,2048]{2,1,0:T(8,128)(2,1)}), bf16[16,11,2048]{2,1,0:T(8,128)(2,1)S(1)}, u32[]{:S(2)}, u32[]{:S(2)}) async-start(bf16[16,11,2048]{2,1,0:T(8,128)(2,1)} %reshape.111), calls=%async_computation.2 | async-start | bytes 2097152 | tf_op jit(solution)/shard_map/all_to_all | solution.py:79
  20.0 64.0 %all-gather.7.cloned.1.call-start = ((), (), s32[]{:S(2)}) async-start(), calls=%async_computation.10 | async-start | bytes 4718592 | tf_op jit(solution)/shard_map/all_gather | solution.py:88
  21.5 26.0 %copy-start.14 = (f32[16]{0:T(128)}, f32[16]{0:T(128)S(1)}, u32[]{:S(2)}) copy-start(f32[16]{0:T(128)S(1)} %get-tuple-element.17) | copy-start | bytes 196
  47.5 30.5 %all-to-all-start = ((bf16[16,11,2048]{2,1,0:T(8,128)(2,1)}), bf16[16,11,2048]{2,1,0:T(8,128)(2,1)S(1)}, u32[]{:S(2)}, u32[]{:S(2)}) async-start(bf16[16,11,2048]{2,1,0:T(8,128)(2,1)} %reshape.107), calls=%async_computation | async-start | bytes 2097152 | tf_op jit(solution)/shard_map/all_to_all | solution.py:72
  51.2 140.6 %reduce-scatter.8.cloned.1.call-start = ((), (), s32[]{:S(2)}) async-start(), calls=%async_computation.9 | async-start | bytes 9437184 | tf_op jit(solution)/shard_map/reduce_scatter | solution.py:102
  86.9 3.7 %copy-start.2 = (bf16[176,768]{1,0:T(8,128)(2,1)}, bf16[176,768]{1,0:T(8,128)(2,1)S(1)}, u32[]{:S(2)}) copy-start(bf16[176,768]{1,0:T(8,128)(2,1)S(1)} %get-tuple-element.11) | copy-start | bytes 811012
  86.9 7.8 %copy-start.4 = (bf16[176,768]{1,0:T(8,128)(2,1)}, bf16[176,768]{1,0:T(8,128)(2,1)S(1)}, u32[]{:S(2)}) copy-start(bf16[176,768]{1,0:T(8,128)(2,1)S(1)} %get-tuple-element.12) | copy-start | bytes 811012
  90.5 104.6 %reduce-scatter.4.cloned.1.call-start = ((), (), s32[]{:S(2)}) async-start(), calls=%async_computation.7 | async-start | bytes 9437184 | tf_op jit(solution)/shard_map/reduce_scatter | solution.py:100
  94.6 103.7 %reduce-scatter.6.cloned.1.call-start = ((), (), s32[]{:S(2)}) async-start(), calls=%async_computation.8 | async-start | bytes 9437184 | tf_op jit(solution)/shard_map/reduce_scatter | solution.py:101
  99.5 10.7 %copy-start = (bf16[1,2048,768]{2,1,0:T(8,128)(2,1)S(1)}, bf16[1,2048,768]{2,1,0:T(8,128)(2,1)}, u32[]{:S(2)}) copy-start(bf16[1,2048,768]{2,1,0:T(8,128)(2,1)} %all-gather.9.cloned.1.call-done) | copy-start | bytes 9437188
  105.7 6.8 %copy-start.3 = (bf16[176,768]{1,0:T(8,128)(2,1)S(1)}, bf16[176,768]{1,0:T(8,128)(2,1)}, u32[]{:S(2)}) copy-start(bf16[176,768]{1,0:T(8,128)(2,1)} %copy-done.2) | copy-start | bytes 811012
  105.7 30.7 %all-to-all-start.1 = ((bf16[16,11,2048]{2,1,0:T(8,128)(2,1)}), bf16[16,11,2048]{2,1,0:T(8,128)(2,1)}, u32[]{:S(2)}, u32[]{:S(2)}) async-start(bf16[16,11,2048]{2,1,0:T(8,128)(2,1)} %reshape.109), calls=%async_computation.1 | async-start | bytes 2097152 | tf_op jit(solution)/shard_map/all_to_all | solution.py:107
  110.2 2.3 %copy-start.1 = (bf16[1,2048,768]{2,1,0:T(8,128)(2,1)S(1)}, bf16[1,2048,768]{2,1,0:T(8,128)(2,1)}, u32[]{:S(2)}) copy-start(bf16[1,2048,768]{2,1,0:T(8,128)(2,1)} %all-gather.7.cloned.1.call-done) | copy-start | bytes 9437188
  113.7 28.1 %copy-start.11 = (s32[16,8]{1,0:T(8,128)S(1)}, s32[16,8]{1,0:T(8,128)}, u32[]{:S(2)}) copy-start(s32[16,8]{1,0:T(8,128)} %copy-done.10) | copy-start | bytes 1540
  113.7 28.1 %copy-start.13 = (f32[16,8]{1,0:T(8,128)S(1)}, f32[16,8]{1,0:T(8,128)}, u32[]{:S(2)}) copy-start(f32[16,8]{1,0:T(8,128)} %copy-done.12) | copy-start | bytes 1540
  136.4 30.4 %all-to-all-start.3 = ((bf16[16,11,2048]{2,1,0:T(8,128)(2,1)}), bf16[16,11,2048]{2,1,0:T(8,128)(2,1)S(1)}, u32[]{:S(2)}, u32[]{:S(2)}) async-start(bf16[16,11,2048]{2,1,0:T(8,128)(2,1)} %reshape.113), calls=%async_computation.3 | async-start | bytes 2097152 | tf_op jit(solution)/shard_map/all_to_all | solution.py:114
  140.3 26.8 %copy-start.9 = (bf16[16,176]{1,0:T(8,128)(2,1)S(1)}, bf16[16,176]{1,0:T(8,128)(2,1)}, u32[]{:S(2)}) copy-start(bf16[16,176]{1,0:T(8,128)(2,1)} %copy-done.8) | copy-start | bytes 16900
  140.3 26.8 %copy-start.15 = (f32[16]{0:T(128)S(1)}, f32[16]{0:T(128)}, u32[]{:S(2)}) copy-start(f32[16]{0:T(128)} %copy-done.14) | copy-start | bytes 196
  141.8 49.3 %copy-start.18 = (f32[16]{0:T(128)S(1)}, f32[16]{0:T(128)}, u32[]{:S(2)}) copy-start(f32[16]{0:T(128)} %get-tuple-element.16) | copy-start | bytes 196
Sparse Core Ops, SparseCore 0:
  9.6 14.8 all-gather.10
  26.0 13.1 all-gather.8
  40.8 13.1 all-gather.6
  90.6 11.2 reduce-scatter.7
  104.1 15.8 reduce-scatter.3
  122.1 15.0 reduce-scatter.5
